TPU v7x, 128 devices: a whole 4x4x4 slice. The times are simulated.
128 devices in a mesh: wide: 32 (over x, y, z_lo), narrow: 4 (over z_hi, core).
Axes of the slice: x: 4, y: 4, z: 4 (z_hi: 2, z_lo: 2; z = z_hi * 2 + z_lo), core: 2. Of those that a mesh axis runs over, the one named last changes fastest.
Arguments:
- mlp_input: bfloat16 [768, 5120], P('wide', 'narrow'), may hold values from -6 to 6
- grad_rows: bfloat16 [768, 5120], P('wide', 'narrow'), may hold values from -18 to 18
- enc_weight: bfloat16 [5120, 65536], P('narrow', 'wide'), may hold values from -0.078125 to 0.078125
- enc_bias: float32 [65536], P('wide'), may hold values from -3 to 3
- dec_weight: bfloat16 [65536, 5120], P('wide', 'narrow'), may hold values from -0.0234375 to 0.0234375
- dec_bias: float32 [5120], P('narrow'), may hold values from -3 to 3
Outputs:
- recon: bfloat16 [768, 5120], P('wide', 'narrow')
- attribution: bfloat16 [768, 65536], P(None, 'wide')
All inputs are finite; a program needn't handle non-finite values.
Results may differ from a plain program's by a relative error of at most 0.023.
Values may be sent and summed in bfloat16 or wider, within the bound.
No kernel may reach another device: no remote copies, remote signals or barrier semaphores. Data moves between devices by JAX's collectives and lax.ppermute only.
A program may use at most 64 MiB of HBM per device.

v0:
```python
import jax
import jax.numpy as jnp
from jax import lax
from jax.sharding import PartitionSpec as P


def local(mlp_input, grad_rows, enc_weight, enc_bias, dec_weight, dec_bias):
    enc_terms = jnp.dot(
        lax.all_gather(mlp_input, "wide", axis=0, tiled=True),
        enc_weight,
        preferred_element_type=jnp.float32,
    )
    grad_terms = lax.dot_general(
        lax.all_gather(grad_rows, "wide", axis=0, tiled=True),
        dec_weight,
        (((1,), (1,)), ((), ())),
        preferred_element_type=jnp.float32,
    )
    pre, grad_proj = (
        lax.psum(enc_terms.astype(jnp.bfloat16), "narrow").astype(jnp.float32),
        lax.psum(grad_terms.astype(jnp.bfloat16), "narrow").astype(jnp.float32),
    )
    latents = jnp.maximum(pre + enc_bias[None, :], 0.0).astype(jnp.bfloat16)
    attribution = (latents.astype(jnp.float32) * grad_proj).astype(jnp.bfloat16)
    recon_sum = lax.psum_scatter(
        jnp.dot(latents, dec_weight, preferred_element_type=jnp.float32).astype(jnp.bfloat16),
        "wide",
        scatter_dimension=0,
        tiled=True,
    ).astype(jnp.float32)
    recon = (recon_sum + dec_bias[None, :]).astype(jnp.bfloat16)
    return (recon, attribution)


def solution(mesh):
    placed = (
        P("wide", "narrow"),
        P("wide", "narrow"),
        P("narrow", "wide"),
        P("wide"),
        P("wide", "narrow"),
        P("narrow"),
    )
    return jax.shard_map(
        local,
        mesh=mesh,
        in_specs=placed,
        out_specs=(P("wide", "narrow"), P(None, "wide")),
        check_vma=False,
    )
```

profile of v0, /device:TPU:0, one launch (start us, length us, event | category | flops | bytes accessed | tf_op | source)
XLA Modules:
  0.0 636.6 jit_solution(16167423434379626418)
XLA Ops:
  7.2 0.0 all-gather.5.cloned.1.call-start
  7.2 0.7 all-gather.5.cloned.1.call-update
  7.9 0.0 all-gather.3.cloned.1.call-start
  7.9 0.7 all-gather.3.cloned.1.call-update
  8.6 0.0 all-reduce.3.cloned.1.call-start
  8.7 155.7 %all-gather.5.cloned.1.call-done = bf16[768,1280]{1,0:T(8,128)(2,1)} async-done(((bf16[24,1280]{1,0:T(8,128)(2,1)}), bf16[768,1280]{1,0:T(8,128)(2,1)}) %all-gather.5.cloned.1.call-update) | async-done | bytes 1966096 | tf_op jit(solution)/shard_map/all_gather | solution.py:14
  164.4 9.1 %convolution_convert_fusion = bf16[768,2048]{1,0:T(8,128)(2,1)} fusion(bf16[768,1280]{1,0:T(8,128)(2,1)} %all-gather.5.cloned.1.call-done, bf16[2048,1280]{1,0:T(8,128)(2,1)} %param.10), kind=kOutput, calls=%fused_computation.2 | convolution fusion | flops 4028104704 | bytes 10354688 | tf_op jit(solution)/shard_map/dot_general | solution.py:13
  173.4 145.1 %all-gather.3.cloned.1.call-done = bf16[768,1280]{1,0:T(8,128)(2,1)} async-done(((bf16[24,1280]{1,0:T(8,128)(2,1)}), bf16[768,1280]{1,0:T(8,128)(2,1)}) %all-gather.3.cloned.1.call-update) | async-done | bytes 1966096 | tf_op jit(solution)/shard_map/all_gather | solution.py:9
  318.5 9.0 %convolution_convert_fusion.2 = bf16[768,2048]{1,0:T(8,128)(2,1)} fusion(bf16[768,1280]{1,0:T(8,128)(2,1)} %all-gather.3.cloned.1.call-done, bf16[1280,2048]{1,0:T(8,128)(2,1)} %param.8), kind=kOutput, calls=%fused_computation.4 | convolution fusion | flops 4028104704 | bytes 10354688 | tf_op jit(solution)/shard_map/dot_general | solution.py:8
  327.5 0.0 copy-start.2
  327.5 0.0 all-reduce.3.cloned.1.call-update
  327.5 0.0 reduce-scatter.2.cloned.1.call-start
  327.6 127.1 %all-reduce.3.cloned.1.call-done = (bf16[768,2048]{1,0:T(8,128)(2,1)}, bf16[768,2048]{1,0:T(8,128)(2,1)}) async-done(((bf16[768,2048]{1,0:T(8,128)(2,1)}, bf16[768,2048]{1,0:T(8,128)(2,1)}), (bf16[768,2048]{1,0:T(8,128)(2,1)}, bf16[768,2048]{1,0:T(8,128)(2,1)})) %all-reduce.3.cloned.1.call-update) | async-done | bytes 6291472 | tf_op jit(solution)/shard_map/psum | solution.py:20
  454.7 0.0 copy-done.2
  454.7 0.0 copy-start
  454.7 9.1 %convolution_convert_fusion.1 = bf16[768,1280]{1,0:T(8,128)(2,1)} fusion(bf16[2048,1280]{1,0:T(8,128)(2,1)} %param.10, bf16[768,2048]{1,0:T(8,128)(2,1)} %get-tuple-element.2, f32[2048]{0:T(1024)S(1)} %copy-done.2), kind=kOutput, calls=%fused_computation.3 | convolution fusion | flops 4033806336 | bytes 10362880 | tf_op jit(solution)/shard_map/dot_general | solution.py:26
  463.8 0.0 copy-start.1
  463.8 0.0 reduce-scatter.2.cloned.1.call-update
  463.8 0.0 copy-done
  463.8 5.0 multiply_convert_fusion
  468.9 159.7 %reduce-scatter.2.cloned.1.call-done = bf16[24,1280]{1,0:T(8,128)(2,1)} async-done(((bf16[768,1280]{1,0:T(8,128)(2,1)}), bf16[24,1280]{1,0:T(8,128)(2,1)}) %reduce-scatter.2.cloned.1.call-update) | async-done | bytes 61456 | tf_op jit(solution)/shard_map/reduce_scatter | solution.py:25
  628.6 0.0 copy-done.1
  628.6 1.5 add_convert_fusion
Async XLA Ops:
  7.2 157.2 %all-gather.5.cloned.1.call-start = ((), (), s32[]{:S(2)}) async-start(), calls=%async_computation.3 | async-start | bytes 2027520 | tf_op jit(solution)/shard_map/all_gather | solution.py:14
  7.9 310.6 %all-gather.3.cloned.1.call-start = ((), (), s32[]{:S(2)}) async-start(), calls=%async_computation.1 | async-start | bytes 2027520 | tf_op jit(solution)/shard_map/all_gather | solution.py:9
  8.6 446.0 %all-reduce.3.cloned.1.call-start = ((), (), s32[]{:S(2)}) async-start(), calls=%async_computation.4 | async-start | bytes 12582912 | tf_op jit(solution)/shard_map/psum | solution.py:20
  327.5 127.2 %copy-start.2 = (f32[2048]{0:T(1024)S(1)}, f32[2048]{0:T(1024)}, u32[]{:S(2)}) copy-start(f32[2048]{0:T(1024)} %param.9) | copy-start | bytes 24580
  327.5 301.0 %reduce-scatter.2.cloned.1.call-start = ((), (), s32[]{:S(2)}) async-start(), calls=%async_computation.2 | async-start | bytes 2027520 | tf_op jit(solution)/shard_map/reduce_scatter | solution.py:25
  454.7 9.1 %copy-start = (bf16[768,2048]{1,0:T(8,128)(2,1)S(1)}, bf16[768,2048]{1,0:T(8,128)(2,1)}, u32[]{:S(2)}) copy-start(bf16[768,2048]{1,0:T(8,128)(2,1)} %get-tuple-element.2) | copy-start | bytes 9437188
  463.8 164.7 %copy-start.1 = (f32[1280]{0:T(1024)S(1)}, f32[1280]{0:T(1024)}, u32[]{:S(2)}) copy-start(f32[1280]{0:T(1024)} %param.11) | copy-start | bytes 15364
Sparse Core Ops, SparseCore 0:
  9.6 154.7 all-gather.4
  166.0 152.4 all-gather.2
  327.7 126.9 all-reduce.2
  464.0 164.5 reduce-scatter.1
where the time goes:
time: 637 us
  waiting for transfers between devices  589 us (92%)
  matrix products  27.1 us (4%)
  between operations  13.8 us (2%)
  other arithmetic  6.51 us (1%)
    reduce_scatter x1, waiting for transfers between devices, local(): lax.psum_scatter(jnp.dot(latents, dec_weight, preferred_element_type=jnp....  160 us
    all_gather x1, waiting for transfers between devices, local(): lax.all_gather(grad_rows, 'wide', axis=0, tiled=True)  156 us
    all_gather x1, waiting for transfers between devices, local(): lax.all_gather(mlp_input, 'wide', axis=0, tiled=True)  145 us
    psum x1, waiting for transfers between devices, local(): lax.psum(enc_terms.astype(jnp.bfloat16), 'narrow').astype(jnp.float32)  127 us
  transfers between devices with their start and end apart: 4, of which 4 were waited for; matrix products, arithmetic and copies ran while one was open for 2% of the time, Pallas kernels for 0%

commit v1 on v0

--- a/solution.py
+++ b/solution.py
@@ -6,7 +6,9 @@
 
 def local(mlp_input, grad_rows, enc_weight, enc_bias, dec_weight, dec_bias):
     enc_terms = jnp.dot(
-        lax.all_gather(mlp_input, "wide", axis=0, tiled=True),
+        jnp.concatenate(
+            lax.all_to_all(jnp.stack([mlp_input] * lax.axis_size("wide")), "wide", 0, 0), axis=0
+        ),
         enc_weight,
         preferred_element_type=jnp.float32,
     )

time: 637 us -> 498 us (0.78)
  waiting for transfers between devices: 589 us -> 416 us
  blocking collectives: 0 us -> 36.1 us
    all_gather x1 -> x0, waiting for transfers between devices: 145 us -> none  [local(): lax.all_gather(mlp_input, 'wide', axis=0, tiled=True)]
    all_to_all x0 -> x1, blocking collectives: none -> 36.1 us  [local(): lax.all_to_all(jnp.stack([mlp_input] * lax.axis_size('wide')), 'wide', 0, 0)]
    all_gather x1, waiting for transfers between devices: 156 us -> 130 us  [local(): lax.all_gather(grad_rows, 'wide', axis=0, tiled=True)]
  transfers between devices with their start and end apart: 4 -> 3, of which waited for: 4 -> 3; matrix products, arithmetic and copies ran while one was open for 2% -> 2% of each run, Pallas kernels for 0% -> 0%
where the time goes in v1:
time: 498 us
  waiting for transfers between devices  416 us (84%)
  blocking collectives  36.1 us (7%)
  matrix products  23.7 us (5%)
  between operations  13.8 us (3%)
  other arithmetic  6.6 us (1%)
    reduce_scatter x1, waiting for transfers between devices, local(): lax.psum_scatter(jnp.dot(latents, dec_weight, preferred_element_type=jnp....  159 us
    all_gather x1, waiting for transfers between devices, local(): lax.all_gather(grad_rows, 'wide', axis=0, tiled=True)  130 us
    psum x1, waiting for transfers between devices, local(): lax.psum(enc_terms.astype(jnp.bfloat16), 'narrow').astype(jnp.float32)  126 us
    all_to_all x1, blocking collectives, local(): lax.all_to_all(jnp.stack([mlp_input] * lax.axis_size('wide')), 'wide', 0, 0)  36.1 us
  transfers between devices with their start and end apart: 3, of which 3 were waited for; matrix products, arithmetic and copies ran while one was open for 2% of the time, Pallas kernels for 0%

profile of v1, /device:TPU:0, one launch (start us, length us, event | category | flops | bytes accessed | tf_op | source)
XLA Modules:
  0.0 497.7 jit_solution(10654329607562960262)
XLA Ops:
  7.2 0.0 all-gather.2.cloned.1.call-start
  7.2 0.7 all-gather.2.cloned.1.call-update
  7.9 0.0 all-reduce.3.cloned.1.call-start
  7.9 0.0 copy-start.3
  8.0 1.1 stack.2
  9.1 36.1 %all_to_all.5 = bf16[32,24,1280]{2,1,0:T(8,128)(2,1)S(1)} all-to-all(bf16[32,24,1280]{2,1,0:T(8,128)(2,1)S(1)} %stack.2), channel_id=1, replica_groups=mesh['wide'=32,'narrow'=4] {'wide'}, dimensions={0} | all-to-all | bytes 3932160 | tf_op jit(solution)/shard_map/all_to_all | solution.py:10
  45.1 0.0 copy-done.3
  45.1 5.5 %convolution_convert_fusion.2 = bf16[768,2048]{1,0:T(8,128)(2,1)} fusion(bf16[768,1280]{1,0:T(8,128)(2,1)S(1)} %bitcast.6, bf16[1280,2048]{1,0:T(8,128)(2,1)S(1)} %copy-done.3), kind=kOutput, calls=%fused_computation.4 | convolution fusion | flops 4028104704 | bytes 10354688 | tf_op jit(solution)/shard_map/dot_general | solution.py:8
  50.7 130.1 %all-gather.2.cloned.1.call-done = bf16[768,1280]{1,0:T(8,128)(2,1)} async-done(((bf16[24,1280]{1,0:T(8,128)(2,1)}), bf16[768,1280]{1,0:T(8,128)(2,1)}) %all-gather.2.cloned.1.call-update) | async-done | bytes 1966096 | tf_op jit(solution)/shard_map/all_gather | solution.py:16
  180.8 9.0 %convolution_convert_fusion = bf16[768,2048]{1,0:T(8,128)(2,1)} fusion(bf16[768,1280]{1,0:T(8,128)(2,1)} %all-gather.2.cloned.1.call-done, bf16[2048,1280]{1,0:T(8,128)(2,1)} %param.10), kind=kOutput, calls=%fused_computation.2 | convolution fusion | flops 4028104704 | bytes 10354688 | tf_op jit(solution)/shard_map/dot_general | solution.py:15
  189.8 0.0 copy-start.2
  189.8 0.0 all-reduce.3.cloned.1.call-update
  189.8 0.0 reduce-scatter.2.cloned.1.call-start
  189.9 126.3 %all-reduce.3.cloned.1.call-done = (bf16[768,2048]{1,0:T(8,128)(2,1)}, bf16[768,2048]{1,0:T(8,128)(2,1)}) async-done(((bf16[768,2048]{1,0:T(8,128)(2,1)}, bf16[768,2048]{1,0:T(8,128)(2,1)}), (bf16[768,2048]{1,0:T(8,128)(2,1)}, bf16[768,2048]{1,0:T(8,128)(2,1)})) %all-reduce.3.cloned.1.call-update) | async-done | bytes 6291472 | tf_op jit(solution)/shard_map/psum | solution.py:22
  316.2 0.0 copy-done.2
  316.2 0.0 copy-start
  316.2 9.1 %convolution_convert_fusion.1 = bf16[768,1280]{1,0:T(8,128)(2,1)} fusion(bf16[2048,1280]{1,0:T(8,128)(2,1)} %param.10, bf16[768,2048]{1,0:T(8,128)(2,1)} %get-tuple-element.2, f32[2048]{0:T(1024)S(1)} %copy-done.2), kind=kOutput, calls=%fused_computation.3 | convolution fusion | flops 4033806336 | bytes 10362880 | tf_op jit(solution)/shard_map/dot_general | solution.py:28
  325.3 0.0 reduce-scatter.2.cloned.1.call-update
  325.4 0.0 copy-done
  325.4 0.0 copy-start.1
  325.4 5.1 %multiply_convert_fusion = bf16[768,2048]{1,0:T(8,128)(2,1)} fusion(bf16[768,2048]{1,0:T(8,128)(2,1)} %get-tuple-element.3, f32[2048]{0:T(1024)S(1)} %copy-done.2, bf16[768,2048]{1,0:T(8,128)(2,1)S(1)} %copy-done), kind=kLoop, calls=%fused_computation | loop fusion | flops 12582912 | bytes 9445376 | tf_op jit(solution)/shard_map/convert_element_type | solution.py:26
  330.5 159.2 %reduce-scatter.2.cloned.1.call-done = bf16[24,1280]{1,0:T(8,128)(2,1)} async-done(((bf16[768,1280]{1,0:T(8,128)(2,1)}), bf16[24,1280]{1,0:T(8,128)(2,1)}) %reduce-scatter.2.cloned.1.call-update) | async-done | bytes 61456 | tf_op jit(solution)/shard_map/reduce_scatter | solution.py:27
  489.7 0.0 copy-done.1
  489.7 1.5 add_convert_fusion
Async XLA Ops:
  7.2 173.6 %all-gather.2.cloned.1.call-start = ((), (), s32[]{:S(2)}) async-start(), calls=%async_computation.3 | async-start | bytes 2027520 | tf_op jit(solution)/shard_map/all_gather | solution.py:16
  7.9 308.3 %all-reduce.3.cloned.1.call-start = ((), (), s32[]{:S(2)}) async-start(), calls=%async_computation.4 | async-start | bytes 12582912 | tf_op jit(solution)/shard_map/psum | solution.py:22
  7.9 37.2 %copy-start.3 = (bf16[1280,2048]{1,0:T(8,128)(2,1)S(1)}, bf16[1280,2048]{1,0:T(8,128)(2,1)}, u32[]{:S(2)}) copy-start(bf16[1280,2048]{1,0:T(8,128)(2,1)} %param.8) | copy-start | bytes 15728644
  189.8 126.4 %copy-start.2 = (f32[2048]{0:T(1024)S(1)}, f32[2048]{0:T(1024)}, u32[]{:S(2)}) copy-start(f32[2048]{0:T(1024)} %param.9) | copy-start | bytes 24580
  189.8 299.9 %reduce-scatter.2.cloned.1.call-start = ((), (), s32[]{:S(2)}) async-start(), calls=%async_computation.2 | async-start | bytes 2027520 | tf_op jit(solution)/shard_map/reduce_scatter | solution.py:27
  316.2 9.1 %copy-start = (bf16[768,2048]{1,0:T(8,128)(2,1)S(1)}, bf16[768,2048]{1,0:T(8,128)(2,1)}, u32[]{:S(2)}) copy-start(bf16[768,2048]{1,0:T(8,128)(2,1)} %get-tuple-element.2) | copy-start | bytes 9437188
  325.4 164.3 %copy-start.1 = (f32[1280]{0:T(1024)S(1)}, f32[1280]{0:T(1024)}, u32[]{:S(2)}) copy-start(f32[1280]{0:T(1024)} %param.11) | copy-start | bytes 15364
Sparse Core Ops, SparseCore 0:
  9.6 171.1 all-gather.1
  190.0 126.2 all-reduce.2
  325.5 164.1 reduce-scatter.1

commit v2 on v0

--- a/solution.py
+++ b/solution.py
@@ -17,7 +17,9 @@
         preferred_element_type=jnp.float32,
     )
     pre, grad_proj = (
-        lax.psum(enc_terms.astype(jnp.bfloat16), "narrow").astype(jnp.float32),
+        jnp.sum(lax.all_gather(enc_terms.astype(jnp.bfloat16), "narrow"), axis=0).astype(
+            jnp.float32
+        ),
         lax.psum(grad_terms.astype(jnp.bfloat16), "narrow").astype(jnp.float32),
     )
     latents = jnp.maximum(pre + enc_bias[None, :], 0.0).astype(jnp.bfloat16)

time: 637 us -> 659 us (1.035)
  waiting for transfers between devices: 589 us -> 603 us
  other arithmetic: 6.51 us -> 15.4 us
    all_gather x0 -> x1, waiting for transfers between devices: none -> 79.6 us  [local(): lax.all_gather(enc_terms.astype(jnp.bfloat16), 'narrow')]
    psum x1, waiting for transfers between devices: 127 us -> 59.8 us  [local(): lax.psum(grad_terms.astype(jnp.bfloat16), 'narrow').astype(jnp.float32)]
    all_gather x1, waiting for transfers between devices: 156 us -> 145 us  [local(): lax.all_gather(grad_rows, 'wide', axis=0, tiled=True)]
    all_gather x1, waiting for transfers between devices: 145 us -> 156 us  [local(): lax.all_gather(mlp_input, 'wide', axis=0, tiled=True)]
    reduce_sum x0 -> x1, other arithmetic: none -> 8.9 us  [local(): jnp.sum(lax.all_gather(enc_terms.astype(jnp.bfloat16), 'narrow'), axis=0)]
  transfers between devices with their start and end apart: 4 -> 5, of which waited for: 4 -> 5; matrix products, arithmetic and copies ran while one was open for 2% -> 6% of each run, Pallas kernels for 0% -> 0%
where the time goes in v2:
time: 659 us
  waiting for transfers between devices  603 us (92%)
  matrix products  26.5 us (4%)
  other arithmetic  15.4 us (2%)
  between operations  13.8 us (2%)
    reduce_scatter x1, waiting for transfers between devices, local(): lax.psum_scatter(jnp.dot(latents, dec_weight, preferred_element_type=jnp....  161 us
    all_gather x1, waiting for transfers between devices, local(): lax.all_gather(mlp_input, 'wide', axis=0, tiled=True)  156 us
    all_gather x1, waiting for transfers between devices, local(): lax.all_gather(grad_rows, 'wide', axis=0, tiled=True)  145 us
    all_gather x1, waiting for transfers between devices, local(): lax.all_gather(enc_terms.astype(jnp.bfloat16), 'narrow')  79.6 us
    psum x1, waiting for transfers between devices, local(): lax.psum(grad_terms.astype(jnp.bfloat16), 'narrow').astype(jnp.float32)  59.8 us
  transfers between devices with their start and end apart: 5, of which 5 were waited for; matrix products, arithmetic and copies ran while one was open for 6% of the time, Pallas kernels for 0%

profile of v2, /device:TPU:0, one launch (start us, length us, event | category | flops | bytes accessed | tf_op | source)
XLA Modules:
  0.0 658.9 jit_solution(9086583643154458957)
XLA Ops:
  7.2 0.0 all-gather.5.cloned.1.call-start
  7.2 0.7 all-gather.5.cloned.1.call-update
  7.9 0.0 all-gather.7.cloned.1.call-start
  7.9 0.7 all-gather.7.cloned.1.call-update
  8.6 0.0 all-gather.9.cloned.1.call-start
  8.7 155.7 %all-gather.5.cloned.1.call-done = bf16[768,1280]{1,0:T(8,128)(2,1)} async-done(((bf16[24,1280]{1,0:T(8,128)(2,1)}), bf16[768,1280]{1,0:T(8,128)(2,1)}) %all-gather.5.cloned.1.call-update) | async-done | bytes 1966096 | tf_op jit(solution)/shard_map/all_gather | solution.py:9
  164.4 9.0 %convolution_convert_fusion.2 = bf16[768,2048]{1,0:T(8,128)(2,1)} fusion(bf16[768,1280]{1,0:T(8,128)(2,1)} %all-gather.5.cloned.1.call-done, bf16[1280,2048]{1,0:T(8,128)(2,1)} %param.8), kind=kOutput, calls=%fused_computation.4 | convolution fusion | flops 4028104704 | bytes 10354688 | tf_op jit(solution)/shard_map/dot_general | solution.py:8
  173.4 0.0 all-gather.9.cloned.1.call-update
  173.4 0.0 all-reduce.2.cloned.1.call-start
  173.4 145.1 %all-gather.7.cloned.1.call-done = bf16[768,1280]{1,0:T(8,128)(2,1)} async-done(((bf16[24,1280]{1,0:T(8,128)(2,1)}), bf16[768,1280]{1,0:T(8,128)(2,1)}) %all-gather.7.cloned.1.call-update) | async-done | bytes 1966096 | tf_op jit(solution)/shard_map/all_gather | solution.py:14
  318.5 9.0 %convolution_convert_fusion = bf16[768,2048]{1,0:T(8,128)(2,1)} fusion(bf16[768,1280]{1,0:T(8,128)(2,1)} %all-gather.7.cloned.1.call-done, bf16[2048,1280]{1,0:T(8,128)(2,1)} %param.10), kind=kOutput, calls=%fused_computation.2 | convolution fusion | flops 4028104704 | bytes 10354688 | tf_op jit(solution)/shard_map/dot_general | solution.py:13
  327.5 0.0 all-reduce.2.cloned.1.call-update
  327.5 0.2 reduce-scatter.2.cloned.1.call-start
  327.7 79.6 %all-gather.9.cloned.1.call-done = bf16[3072,2048]{1,0:T(8,128)(2,1)} async-done(((bf16[768,2048]{1,0:T(8,128)(2,1)}), bf16[3072,2048]{1,0:T(8,128)(2,1)}) %all-gather.9.cloned.1.call-update) | async-done | bytes 12582928 | tf_op jit(solution)/shard_map/all_gather | solution.py:20
  407.4 0.0 copy-start.1
  407.4 8.9 %reduce_sum.12 = bf16[768,2048]{1,0:T(8,128)(2,1)S(1)} reduce(bf16[4,768,2048]{2,1,0:T(8,128)(2,1)} %bitcast.6, bf16[]{:T(256)} %constant.1.clone.1), dimensions={0}, to_apply=%region_0.0 | reduce | flops 4718592 | bytes 15728642 | tf_op jit(solution)/shard_map/reduce_sum | solution.py:20
  416.3 0.0 copy-done.1
  416.3 8.5 %convolution_convert_fusion.1 = bf16[768,1280]{1,0:T(8,128)(2,1)} fusion(bf16[2048,1280]{1,0:T(8,128)(2,1)} %param.10, bf16[768,2048]{1,0:T(8,128)(2,1)S(1)} %reduce_sum.12, f32[2048]{0:T(1024)S(1)} %copy-done.1), kind=kOutput, calls=%fused_computation.3 | convolution fusion | flops 4033806336 | bytes 10362880 | tf_op jit(solution)/shard_map/dot_general | solution.py:28
  424.8 0.0 copy-start
  424.8 0.0 reduce-scatter.2.cloned.1.call-update
  424.8 59.8 %all-reduce.2.cloned.1.call-done = bf16[768,2048]{1,0:T(8,128)(2,1)} async-done(((bf16[768,2048]{1,0:T(8,128)(2,1)}), bf16[768,2048]{1,0:T(8,128)(2,1)}) %all-reduce.2.cloned.1.call-update) | async-done | bytes 3145744 | tf_op jit(solution)/shard_map/psum | solution.py:23
  484.6 5.0 multiply_convert_fusion
  489.6 161.2 %reduce-scatter.2.cloned.1.call-done = bf16[24,1280]{1,0:T(8,128)(2,1)} async-done(((bf16[768,1280]{1,0:T(8,128)(2,1)}), bf16[24,1280]{1,0:T(8,128)(2,1)}) %reduce-scatter.2.cloned.1.call-update) | async-done | bytes 61456 | tf_op jit(solution)/shard_map/reduce_scatter | solution.py:27
  650.9 0.0 copy-done
  650.9 1.5 add_convert_fusion
Async XLA Ops:
  7.2 157.2 %all-gather.5.cloned.1.call-start = ((), (), s32[]{:S(2)}) async-start(), calls=%async_computation.1 | async-start | bytes 2027520 | tf_op jit(solution)/shard_map/all_gather | solution.py:9
  7.9 310.6 %all-gather.7.cloned.1.call-start = ((), (), s32[]{:S(2)}) async-start(), calls=%async_computation.3 | async-start | bytes 2027520 | tf_op jit(solution)/shard_map/all_gather | solution.py:14
  8.6 398.7 %all-gather.9.cloned.1.call-start = ((), (), s32[]{:S(2)}) async-start(), calls=%async_computation.5 | async-start | bytes 15728640 | tf_op jit(solution)/shard_map/all_gather | solution.py:20
  173.4 311.3 %all-reduce.2.cloned.1.call-start = ((), (), s32[]{:S(2)}) async-start(), calls=%async_computation.4 | async-start | bytes 6291456 | tf_op jit(solution)/shard_map/psum | solution.py:23
  327.5 323.4 %reduce-scatter.2.cloned.1.call-start = ((), (), s32[]{:S(2)}) async-start(), calls=%async_computation.2 | async-start | bytes 2027520 | tf_op jit(solution)/shard_map/reduce_scatter | solution.py:27
  407.4 8.9 %copy-start.1 = (f32[2048]{0:T(1024)S(1)}, f32[2048]{0:T(1024)}, u32[]{:S(2)}) copy-start(f32[2048]{0:T(1024)} %param.9) | copy-start | bytes 24580
  424.8 226.1 %copy-start = (f32[1280]{0:T(1024)S(1)}, f32[1280]{0:T(1024)}, u32[]{:S(2)}) copy-start(f32[1280]{0:T(1024)} %param.11) | copy-start | bytes 15364
Sparse Core Ops, SparseCore 0:
  9.6 154.7 all-gather.4
  166.0 152.4 all-gather.6
  320.7 86.5 all-gather.8
  409.7 74.8 all-reduce.1
  486.9 163.9 reduce-scatter.1
